TPU v7x, 32 devices: a whole 2x2x4 slice. The times are simulated.
32 devices in a mesh: dom: 8 (over z, y), rows: 4 (over x, core).
Axes of the slice: x: 2, y: 2, z: 4, core: 2. Of those that a mesh axis runs over, the one named last changes fastest.
Arguments:
- images: bfloat16 [3584, 25600], P('dom', 'rows'), may hold values from -6 to 6
- panels: bfloat16 [16, 25600, 256], P('dom', 'rows')
- mean_panels: float32 [16, 25600], P('dom', 'rows'), may hold values from -6 to 6
- ctf_table: float32 [16, 25600], P(None, 'rows'), may hold values from -1 to 1
- pose_bin: int32 [3584], P('dom'), may hold values from 0 to 1
- ctf_group: int32 [3584], P('dom'), may hold values from 0 to 15
Outputs:
- scores: float32 [3584, 256], P('dom')
- factor: float32 [256, 256], replicated
All inputs are finite; a program needn't handle non-finite values.
Results may differ from a plain program's by a relative error of at most 0.003.
Values sent between devices are 32-bit elements; how exact they have to be, the bound alone decides.
A program may use at most 128 MiB of HBM per device.

v0:
```python
import jax
import jax.numpy as jnp
from jax import lax
from jax.sharding import PartitionSpec as P


def high_dot(left, right):
    return jnp.dot(left, right, precision=lax.Precision.HIGHEST, preferred_element_type=jnp.float32)


def cholesky_small(matrix):
    order = matrix.shape[0]
    places = jnp.arange(order, dtype=jnp.int32)

    def column_step(index, carry):
        work, lower = carry
        index = jnp.asarray(index).astype(jnp.int32)
        column = lax.dynamic_slice_in_dim(work, index, 1, 1)[:, 0]
        pivot = jnp.sqrt(lax.dynamic_slice_in_dim(column, index, 1, 0)[0])
        below = jnp.where(places > index, column / pivot, jnp.zeros_like(column))
        filled = below + jnp.where(places == index, pivot, jnp.zeros_like(column))
        lower = lower + filled[:, None] * (places == index).astype(matrix.dtype)[None, :]
        work = work - below[:, None] * below[None, :]
        return (work, lower)

    return lax.fori_loop(0, order, column_step, (matrix, jnp.zeros_like(matrix)))[1]


def inverse_small(lower):
    order = lower.shape[0]
    places = jnp.arange(order, dtype=jnp.int32)

    def row_step(index, inverse):
        index = jnp.asarray(index).astype(jnp.int32)
        row_lower = lax.dynamic_slice_in_dim(lower, index, 1, 0)[0]
        pivot = lax.dynamic_slice_in_dim(row_lower, index, 1, 0)[0]
        unit = (places == index).astype(lower.dtype)
        solved = (unit - high_dot(row_lower, inverse)) / pivot
        return inverse + unit[:, None] * solved[None, :]

    return lax.fori_loop(0, order, row_step, jnp.zeros_like(lower))


def assemble(top_left, bottom_left, bottom_right):
    half = top_left.shape[0]
    rest = bottom_right.shape[0]
    upper_part = jnp.concatenate([top_left, jnp.zeros((half, rest), top_left.dtype)], axis=1)
    lower_part = jnp.concatenate([bottom_left, bottom_right], axis=1)
    return jnp.concatenate([upper_part, lower_part], axis=0)


def cholesky_pair(matrix):
    order = matrix.shape[0]
    if order <= 16:
        lower = cholesky_small(matrix)
        return (lower, inverse_small(lower))
    half = order // 2
    lower_a, inverse_a = cholesky_pair(matrix[:half, :half])
    below = high_dot(matrix[half:, :half], inverse_a.T)
    schur = matrix[half:, half:] - high_dot(below, below.T)
    lower_b, inverse_b = cholesky_pair(schur)
    inverse_mid = -high_dot(inverse_b, high_dot(below, inverse_a))
    return (assemble(lower_a, below, lower_b), assemble(inverse_a, inverse_mid, inverse_b))


def weighted_rows(images, pose_bin, ctf_group, mean_panels, ctf_table):
    ctf_rows = jnp.take(ctf_table, ctf_group, axis=0)
    mean_rows = jnp.broadcast_to(mean_panels[0][None, :], images.shape)
    mean_rows = jnp.where((pose_bin == 1)[:, None], mean_panels[1][None, :], mean_rows)
    return (ctf_rows * (images.astype(jnp.float32) - ctf_rows * mean_rows)).astype(jnp.bfloat16)


def project(weighted, pose_bin, panels):
    coeffs = jnp.zeros((weighted.shape[0], panels.shape[2]), jnp.float32)
    for which in range(panels.shape[0]):
        chosen = jnp.where((pose_bin == which)[:, None], weighted, jnp.zeros_like(weighted))
        coeffs = coeffs + jnp.dot(chosen, panels[which], preferred_element_type=jnp.float32)
    return coeffs


def gram_of(coeffs):
    return high_dot(coeffs.T, coeffs)


def body(images, panels, mean_panels, ctf_table, pose_bin, ctf_group):
    weighted = weighted_rows(images, pose_bin, ctf_group, mean_panels, ctf_table)
    particles = images.shape[0] * lax.axis_size("dom")
    coeffs = lax.psum(project(weighted, pose_bin, panels), "rows")
    gram = gram_of(coeffs)
    gram = gram / particles
    lower, inverse = cholesky_pair(lax.psum(gram, "dom"))
    factor = lower.T
    scores = jnp.dot(coeffs, inverse.T, precision=lax.Precision.HIGHEST)
    return (scores, factor)


def solution(mesh):
    placed = (
        P("dom", "rows"),
        P("dom", "rows", None),
        P("dom", "rows"),
        P(None, "rows"),
        P("dom"),
        P("dom"),
    )
    return jax.shard_map(
        body, mesh=mesh, in_specs=placed, out_specs=(P("dom", None), P()), check_vma=False
    )
```

profile of v0, /device:TPU:0, one launch (start us, length us, event | category | flops | bytes accessed | tf_op | source)
XLA Modules:
  0.0 915.7 jit_solution(18135375663425104981)
XLA Ops:
  28.9 35.7 %all-reduce.33.cloned.1.call-done = f32[448,256]{1,0:T(8,128)} async-done(((f32[448,256]{1,0:T(8,128)}), f32[448,256]{1,0:T(8,128)}) %all-reduce.33.cloned.1.call-update) | async-done | bytes 458768 | tf_op jit(solution)/shard_map/psum | solution.py:88
  67.8 71.8 %all-reduce.35.cloned.1.call-done = f32[256,256]{1,0:T(8,128)} async-done(((f32[256,256]{1,0:T(8,128)}), f32[256,256]{1,0:T(8,128)}) %all-reduce.35.cloned.1.call-update) | async-done | bytes 262160 | tf_op jit(solution)/shard_map/psum | solution.py:91
  140.4 23.6 %while.608 = (s32[]{:T(128)}, f32[16,16]{0,1:T(8,128)S(1)}, f32[16,16]{1,0:T(8,128)S(1)}, s32[]{:T(128)}, s32[]{:T(128)}, /*index=5*/s32[]{:T(128)}) while((s32[]{:T(128)}, f32[16,16]{0,1:T(8,128)S(1)}, f32[16,16]{1,0:T(8,128)S(1)}, s32[]{:T(128)}, s32[]{:T(128)}, /*index=5*/s32[]{:T(128)}) %tuple.1341), condition=%wide.region_3.4_spmd.clone.clone, body=%wide.region_2.3_spmd.clone.clone.sunk | while | flops 1476 | bytes 7039 | solution.py:26
  164.1 23.2 %while.592 = (s32[]{:T(128)}, f32[16,16]{1,0:T(8,128)S(1)}, f32[16,16]{1,0:T(8,128)S(1)}, s32[]{:T(128)}, s32[]{:T(128)}, /*index=5*/s32[]{:T(128)}) while((s32[]{:T(128)}, f32[16,16]{1,0:T(8,128)S(1)}, f32[16,16]{1,0:T(8,128)S(1)}, s32[]{:T(128)}, s32[]{:T(128)}, /*index=5*/s32[]{:T(128)}) %tuple.1344), condition=%wide.region_5.6_spmd.clone, body=%wide.region_4.5_spmd.clone.sunk | while | flops 4196 | bytes 12656 | solution.py:41
  189.2 23.6 %while.609 = (s32[]{:T(128)}, f32[16,16]{0,1:T(8,128)S(1)}, f32[16,16]{1,0:T(8,128)S(1)}, s32[]{:T(128)}, s32[]{:T(128)}, /*index=5*/s32[]{:T(128)}) while((s32[]{:T(128)}, f32[16,16]{0,1:T(8,128)S(1)}, f32[16,16]{1,0:T(8,128)S(1)}, s32[]{:T(128)}, s32[]{:T(128)}, /*index=5*/s32[]{:T(128)}) %tuple.1347), condition=%wide.region_7.8_spmd.clone.clone, body=%wide.region_6.7_spmd.clone.clone.sunk | while | flops 1476 | bytes 7039 | solution.py:26
  212.8 23.2 %while.593 = (s32[]{:T(128)}, f32[16,16]{1,0:T(8,128)S(1)}, f32[16,16]{1,0:T(8,128)S(1)}, s32[]{:T(128)}, s32[]{:T(128)}, /*index=5*/s32[]{:T(128)}) while((s32[]{:T(128)}, f32[16,16]{1,0:T(8,128)S(1)}, f32[16,16]{1,0:T(8,128)S(1)}, s32[]{:T(128)}, s32[]{:T(128)}, /*index=5*/s32[]{:T(128)}) %tuple.1350), condition=%wide.region_9.10_spmd.clone, body=%wide.region_8.9_spmd.clone.sunk | while | flops 4196 | bytes 12656 | solution.py:41
  238.3 23.6 %while.610 = (s32[]{:T(128)}, f32[16,16]{0,1:T(8,128)S(1)}, f32[16,16]{1,0:T(8,128)S(1)}, s32[]{:T(128)}, s32[]{:T(128)}, /*index=5*/s32[]{:T(128)}) while((s32[]{:T(128)}, f32[16,16]{0,1:T(8,128)S(1)}, f32[16,16]{1,0:T(8,128)S(1)}, s32[]{:T(128)}, s32[]{:T(128)}, /*index=5*/s32[]{:T(128)}) %tuple.1353), condition=%wide.region_11.12_spmd.clone.clone, body=%wide.region_10.11_spmd.clone.clone.sunk | while | flops 1476 | bytes 7039 | solution.py:26
  261.9 23.2 %while.594 = (s32[]{:T(128)}, f32[16,16]{1,0:T(8,128)S(1)}, f32[16,16]{1,0:T(8,128)S(1)}, s32[]{:T(128)}, s32[]{:T(128)}, /*index=5*/s32[]{:T(128)}) while((s32[]{:T(128)}, f32[16,16]{1,0:T(8,128)S(1)}, f32[16,16]{1,0:T(8,128)S(1)}, s32[]{:T(128)}, s32[]{:T(128)}, /*index=5*/s32[]{:T(128)}) %tuple.1356), condition=%wide.region_13.14_spmd.clone, body=%wide.region_12.13_spmd.clone.sunk | while | flops 4196 | bytes 12656 | solution.py:41
  285.6 23.6 %while.611 = (s32[]{:T(128)}, f32[16,16]{0,1:T(8,128)S(1)}, f32[16,16]{1,0:T(8,128)S(1)}, s32[]{:T(128)}, s32[]{:T(128)}, /*index=5*/s32[]{:T(128)}) while((s32[]{:T(128)}, f32[16,16]{0,1:T(8,128)S(1)}, f32[16,16]{1,0:T(8,128)S(1)}, s32[]{:T(128)}, s32[]{:T(128)}, /*index=5*/s32[]{:T(128)}) %tuple.1359), condition=%wide.region_15.16_spmd.clone.clone, body=%wide.region_14.15_spmd.clone.clone.sunk | while | flops 1476 | bytes 7039 | solution.py:26
  309.2 23.2 %while.595 = (s32[]{:T(128)}, f32[16,16]{1,0:T(8,128)S(1)}, f32[16,16]{1,0:T(8,128)S(1)}, s32[]{:T(128)}, s32[]{:T(128)}, /*index=5*/s32[]{:T(128)}) while((s32[]{:T(128)}, f32[16,16]{1,0:T(8,128)S(1)}, f32[16,16]{1,0:T(8,128)S(1)}, s32[]{:T(128)}, s32[]{:T(128)}, /*index=5*/s32[]{:T(128)}) %tuple.1362), condition=%wide.region_17.18_spmd.clone, body=%wide.region_16.17_spmd.clone.sunk | while | flops 4196 | bytes 12656 | solution.py:41
  334.9 23.6 %while.612 = (s32[]{:T(128)}, f32[16,16]{0,1:T(8,128)S(1)}, f32[16,16]{1,0:T(8,128)S(1)}, s32[]{:T(128)}, s32[]{:T(128)}, /*index=5*/s32[]{:T(128)}) while((s32[]{:T(128)}, f32[16,16]{0,1:T(8,128)S(1)}, f32[16,16]{1,0:T(8,128)S(1)}, s32[]{:T(128)}, s32[]{:T(128)}, /*index=5*/s32[]{:T(128)}) %tuple.1365), condition=%wide.region_19.20_spmd.clone.clone, body=%wide.region_18.19_spmd.clone.clone.sunk | while | flops 1476 | bytes 7039 | solution.py:26
  358.5 23.2 %while.596 = (s32[]{:T(128)}, f32[16,16]{1,0:T(8,128)S(1)}, f32[16,16]{1,0:T(8,128)S(1)}, s32[]{:T(128)}, s32[]{:T(128)}, /*index=5*/s32[]{:T(128)}) while((s32[]{:T(128)}, f32[16,16]{1,0:T(8,128)S(1)}, f32[16,16]{1,0:T(8,128)S(1)}, s32[]{:T(128)}, s32[]{:T(128)}, /*index=5*/s32[]{:T(128)}) %tuple.1368), condition=%wide.region_21.22_spmd.clone, body=%wide.region_20.21_spmd.clone.sunk | while | flops 4196 | bytes 12656 | solution.py:41
  382.4 23.6 %while.613 = (s32[]{:T(128)}, f32[16,16]{0,1:T(8,128)S(1)}, f32[16,16]{1,0:T(8,128)S(1)}, s32[]{:T(128)}, s32[]{:T(128)}, /*index=5*/s32[]{:T(128)}) while((s32[]{:T(128)}, f32[16,16]{0,1:T(8,128)S(1)}, f32[16,16]{1,0:T(8,128)S(1)}, s32[]{:T(128)}, s32[]{:T(128)}, /*index=5*/s32[]{:T(128)}) %tuple.1371), condition=%wide.region_23.24_spmd.clone.clone, body=%wide.region_22.23_spmd.clone.clone.sunk | while | flops 1476 | bytes 7039 | solution.py:26
  406.1 23.2 %while.597 = (s32[]{:T(128)}, f32[16,16]{1,0:T(8,128)S(1)}, f32[16,16]{1,0:T(8,128)S(1)}, s32[]{:T(128)}, s32[]{:T(128)}, /*index=5*/s32[]{:T(128)}) while((s32[]{:T(128)}, f32[16,16]{1,0:T(8,128)S(1)}, f32[16,16]{1,0:T(8,128)S(1)}, s32[]{:T(128)}, s32[]{:T(128)}, /*index=5*/s32[]{:T(128)}) %tuple.1374), condition=%wide.region_25.26_spmd.clone, body=%wide.region_24.25_spmd.clone.sunk | while | flops 4196 | bytes 12656 | solution.py:41
  430.1 23.6 %while.614 = (s32[]{:T(128)}, f32[16,16]{0,1:T(8,128)S(1)}, f32[16,16]{1,0:T(8,128)S(1)}, s32[]{:T(128)}, s32[]{:T(128)}, /*index=5*/s32[]{:T(128)}) while((s32[]{:T(128)}, f32[16,16]{0,1:T(8,128)S(1)}, f32[16,16]{1,0:T(8,128)S(1)}, s32[]{:T(128)}, s32[]{:T(128)}, /*index=5*/s32[]{:T(128)}) %tuple.1377), condition=%wide.region_27.28_spmd.clone.clone, body=%wide.region_26.27_spmd.clone.clone.sunk | while | flops 1476 | bytes 7039 | solution.py:26
  453.7 23.2 %while.598 = (s32[]{:T(128)}, f32[16,16]{1,0:T(8,128)S(1)}, f32[16,16]{1,0:T(8,128)S(1)}, s32[]{:T(128)}, s32[]{:T(128)}, /*index=5*/s32[]{:T(128)}) while((s32[]{:T(128)}, f32[16,16]{1,0:T(8,128)S(1)}, f32[16,16]{1,0:T(8,128)S(1)}, s32[]{:T(128)}, s32[]{:T(128)}, /*index=5*/s32[]{:T(128)}) %tuple.1380), condition=%wide.region_29.30_spmd.clone, body=%wide.region_28.29_spmd.clone.sunk | while | flops 4196 | bytes 12656 | solution.py:41
  477.4 23.6 %while.615 = (s32[]{:T(128)}, f32[16,16]{0,1:T(8,128)S(1)}, f32[16,16]{1,0:T(8,128)S(1)}, s32[]{:T(128)}, s32[]{:T(128)}, /*index=5*/s32[]{:T(128)}) while((s32[]{:T(128)}, f32[16,16]{0,1:T(8,128)S(1)}, f32[16,16]{1,0:T(8,128)S(1)}, s32[]{:T(128)}, s32[]{:T(128)}, /*index=5*/s32[]{:T(128)}) %tuple.1383), condition=%wide.region_31.32_spmd.clone.clone, body=%wide.region_30.31_spmd.clone.clone.sunk | while | flops 1476 | bytes 7039 | solution.py:26
  501.0 23.2 %while.599 = (s32[]{:T(128)}, f32[16,16]{1,0:T(8,128)S(1)}, f32[16,16]{1,0:T(8,128)S(1)}, s32[]{:T(128)}, s32[]{:T(128)}, /*index=5*/s32[]{:T(128)}) while((s32[]{:T(128)}, f32[16,16]{1,0:T(8,128)S(1)}, f32[16,16]{1,0:T(8,128)S(1)}, s32[]{:T(128)}, s32[]{:T(128)}, /*index=5*/s32[]{:T(128)}) %tuple.1386), condition=%wide.region_33.34_spmd.clone, body=%wide.region_32.33_spmd.clone.sunk | while | flops 4196 | bytes 12656 | solution.py:41
  525.6 23.6 %while.616 = (s32[]{:T(128)}, f32[16,16]{0,1:T(8,128)S(1)}, f32[16,16]{1,0:T(8,128)S(1)}, s32[]{:T(128)}, s32[]{:T(128)}, /*index=5*/s32[]{:T(128)}) while((s32[]{:T(128)}, f32[16,16]{0,1:T(8,128)S(1)}, f32[16,16]{1,0:T(8,128)S(1)}, s32[]{:T(128)}, s32[]{:T(128)}, /*index=5*/s32[]{:T(128)}) %tuple.1389), condition=%wide.region_35.36_spmd.clone.clone, body=%wide.region_34.35_spmd.clone.clone.sunk | while | flops 1476 | bytes 7039 | solution.py:26
  549.2 23.2 %while.600 = (s32[]{:T(128)}, f32[16,16]{1,0:T(8,128)S(1)}, f32[16,16]{1,0:T(8,128)S(1)}, s32[]{:T(128)}, s32[]{:T(128)}, /*index=5*/s32[]{:T(128)}) while((s32[]{:T(128)}, f32[16,16]{1,0:T(8,128)S(1)}, f32[16,16]{1,0:T(8,128)S(1)}, s32[]{:T(128)}, s32[]{:T(128)}, /*index=5*/s32[]{:T(128)}) %tuple.1392), condition=%wide.region_37.38_spmd.clone, body=%wide.region_36.37_spmd.clone.sunk | while | flops 4196 | bytes 12656 | solution.py:41
  572.9 23.6 %while.617 = (s32[]{:T(128)}, f32[16,16]{0,1:T(8,128)S(1)}, f32[16,16]{1,0:T(8,128)S(1)}, s32[]{:T(128)}, s32[]{:T(128)}, /*index=5*/s32[]{:T(128)}) while((s32[]{:T(128)}, f32[16,16]{0,1:T(8,128)S(1)}, f32[16,16]{1,0:T(8,128)S(1)}, s32[]{:T(128)}, s32[]{:T(128)}, /*index=5*/s32[]{:T(128)}) %tuple.1395), condition=%wide.region_39.40_spmd.clone.clone, body=%wide.region_38.39_spmd.clone.clone.sunk | while | flops 1476 | bytes 7039 | solution.py:26
  596.6 23.2 %while.601 = (s32[]{:T(128)}, f32[16,16]{1,0:T(8,128)S(1)}, f32[16,16]{1,0:T(8,128)S(1)}, s32[]{:T(128)}, s32[]{:T(128)}, /*index=5*/s32[]{:T(128)}) while((s32[]{:T(128)}, f32[16,16]{1,0:T(8,128)S(1)}, f32[16,16]{1,0:T(8,128)S(1)}, s32[]{:T(128)}, s32[]{:T(128)}, /*index=5*/s32[]{:T(128)}) %tuple.1398), condition=%wide.region_41.42_spmd.clone, body=%wide.region_40.41_spmd.clone.sunk | while | flops 4196 | bytes 12656 | solution.py:41
  620.6 23.6 %while.618 = (s32[]{:T(128)}, f32[16,16]{0,1:T(8,128)S(1)}, f32[16,16]{1,0:T(8,128)S(1)}, s32[]{:T(128)}, s32[]{:T(128)}, /*index=5*/s32[]{:T(128)}) while((s32[]{:T(128)}, f32[16,16]{0,1:T(8,128)S(1)}, f32[16,16]{1,0:T(8,128)S(1)}, s32[]{:T(128)}, s32[]{:T(128)}, /*index=5*/s32[]{:T(128)}) %tuple.1401), condition=%wide.region_43.44_spmd.clone.clone, body=%wide.region_42.43_spmd.clone.clone.sunk | while | flops 1476 | bytes 7039 | solution.py:26
  644.2 23.2 %while.602 = (s32[]{:T(128)}, f32[16,16]{1,0:T(8,128)S(1)}, f32[16,16]{1,0:T(8,128)S(1)}, s32[]{:T(128)}, s32[]{:T(128)}, /*index=5*/s32[]{:T(128)}) while((s32[]{:T(128)}, f32[16,16]{1,0:T(8,128)S(1)}, f32[16,16]{1,0:T(8,128)S(1)}, s32[]{:T(128)}, s32[]{:T(128)}, /*index=5*/s32[]{:T(128)}) %tuple.1404), condition=%wide.region_45.46_spmd.clone, body=%wide.region_44.45_spmd.clone.sunk | while | flops 4196 | bytes 12656 | solution.py:41
  667.9 23.6 %while.619 = (s32[]{:T(128)}, f32[16,16]{0,1:T(8,128)S(1)}, f32[16,16]{1,0:T(8,128)S(1)}, s32[]{:T(128)}, s32[]{:T(128)}, /*index=5*/s32[]{:T(128)}) while((s32[]{:T(128)}, f32[16,16]{0,1:T(8,128)S(1)}, f32[16,16]{1,0:T(8,128)S(1)}, s32[]{:T(128)}, s32[]{:T(128)}, /*index=5*/s32[]{:T(128)}) %tuple.1407), condition=%wide.region_47.48_spmd.clone.clone, body=%wide.region_46.47_spmd.clone.clone.sunk | while | flops 1476 | bytes 7039 | solution.py:26
  691.5 23.2 %while.603 = (s32[]{:T(128)}, f32[16,16]{1,0:T(8,128)S(1)}, f32[16,16]{1,0:T(8,128)S(1)}, s32[]{:T(128)}, s32[]{:T(128)}, /*index=5*/s32[]{:T(128)}) while((s32[]{:T(128)}, f32[16,16]{1,0:T(8,128)S(1)}, f32[16,16]{1,0:T(8,128)S(1)}, s32[]{:T(128)}, s32[]{:T(128)}, /*index=5*/s32[]{:T(128)}) %tuple.1410), condition=%wide.region_49.50_spmd.clone, body=%wide.region_48.49_spmd.clone.sunk | while | flops 4196 | bytes 12656 | solution.py:41
  715.7 23.6 %while.620 = (s32[]{:T(128)}, f32[16,16]{0,1:T(8,128)S(1)}, f32[16,16]{1,0:T(8,128)S(1)}, s32[]{:T(128)}, s32[]{:T(128)}, /*index=5*/s32[]{:T(128)}) while((s32[]{:T(128)}, f32[16,16]{0,1:T(8,128)S(1)}, f32[16,16]{1,0:T(8,128)S(1)}, s32[]{:T(128)}, s32[]{:T(128)}, /*index=5*/s32[]{:T(128)}) %tuple.1413), condition=%wide.region_51.52_spmd.clone.clone, body=%wide.region_50.51_spmd.clone.clone.sunk | while | flops 1476 | bytes 7039 | solution.py:26
  739.3 23.2 %while.604 = (s32[]{:T(128)}, f32[16,16]{1,0:T(8,128)S(1)}, f32[16,16]{1,0:T(8,128)S(1)}, s32[]{:T(128)}, s32[]{:T(128)}, /*index=5*/s32[]{:T(128)}) while((s32[]{:T(128)}, f32[16,16]{1,0:T(8,128)S(1)}, f32[16,16]{1,0:T(8,128)S(1)}, s32[]{:T(128)}, s32[]{:T(128)}, /*index=5*/s32[]{:T(128)}) %tuple.1416), condition=%wide.region_53.54_spmd.clone, body=%wide.region_52.53_spmd.clone.sunk | while | flops 4196 | bytes 12656 | solution.py:41
  763.6 23.6 %while.621 = (s32[]{:T(128)}, f32[16,16]{0,1:T(8,128)S(1)}, f32[16,16]{1,0:T(8,128)S(1)}, s32[]{:T(128)}, s32[]{:T(128)}, /*index=5*/s32[]{:T(128)}) while((s32[]{:T(128)}, f32[16,16]{0,1:T(8,128)S(1)}, f32[16,16]{1,0:T(8,128)S(1)}, s32[]{:T(128)}, s32[]{:T(128)}, /*index=5*/s32[]{:T(128)}) %tuple.1419), condition=%wide.region_55.56_spmd.clone.clone, body=%wide.region_54.55_spmd.clone.clone.sunk | while | flops 1476 | bytes 7039 | solution.py:26
  787.3 23.2 %while.605 = (s32[]{:T(128)}, f32[16,16]{1,0:T(8,128)S(1)}, f32[16,16]{1,0:T(8,128)S(1)}, s32[]{:T(128)}, s32[]{:T(128)}, /*index=5*/s32[]{:T(128)}) while((s32[]{:T(128)}, f32[16,16]{1,0:T(8,128)S(1)}, f32[16,16]{1,0:T(8,128)S(1)}, s32[]{:T(128)}, s32[]{:T(128)}, /*index=5*/s32[]{:T(128)}) %tuple.1422), condition=%wide.region_57.58_spmd.clone, body=%wide.region_56.57_spmd.clone.sunk | while | flops 4196 | bytes 12656 | solution.py:41
  811.3 23.6 %while.622 = (s32[]{:T(128)}, f32[16,16]{0,1:T(8,128)S(1)}, f32[16,16]{1,0:T(8,128)S(1)}, s32[]{:T(128)}, s32[]{:T(128)}, /*index=5*/s32[]{:T(128)}) while((s32[]{:T(128)}, f32[16,16]{0,1:T(8,128)S(1)}, f32[16,16]{1,0:T(8,128)S(1)}, s32[]{:T(128)}, s32[]{:T(128)}, /*index=5*/s32[]{:T(128)}) %tuple.1425), condition=%wide.region_59.60_spmd.clone.clone, body=%wide.region_58.59_spmd.clone.clone.sunk | while | flops 1476 | bytes 7039 | solution.py:26
  858.8 23.6 %while.623 = (s32[]{:T(128)}, f32[16,16]{0,1:T(8,128)S(1)}, f32[16,16]{1,0:T(8,128)S(1)}, s32[]{:T(128)}, s32[]{:T(128)}, /*index=5*/s32[]{:T(128)}) while((s32[]{:T(128)}, f32[16,16]{0,1:T(8,128)S(1)}, f32[16,16]{1,0:T(8,128)S(1)}, s32[]{:T(128)}, s32[]{:T(128)}, /*index=5*/s32[]{:T(128)}) %tuple.1431), condition=%wide.region_63.64_spmd.clone.clone, body=%wide.region_62.63_spmd.clone.clone.sunk | while | flops 1476 | bytes 7039 | solution.py:26
  (2980 shorter events, 655.9 us)
Async XLA Ops:
  7.2 2.5 copy-start
  7.2 57.4 %all-reduce.33.cloned.1.call-start = ((), (), s32[]{:S(2)}) async-start(), calls=%async_computation | async-start | bytes 917504 | tf_op jit(solution)/shard_map/psum | solution.py:88
  16.6 7.8 copy-start.3
  28.7 110.9 %all-reduce.35.cloned.1.call-start = ((), (), s32[]{:S(2)}) async-start(), calls=%async_computation.1 | async-start | bytes 524288 | tf_op jit(solution)/shard_map/psum | solution.py:91
  139.6 385.3 %copy-start.2 = (f32[256,256]{1,0:T(8,128)S(1)}, f32[256,256]{1,0:T(8,128)}, u32[]{:S(2)}) copy-start(f32[256,256]{1,0:T(8,128)} %all-reduce.35.cloned.1.call-done) | copy-start | bytes 786436
  501.0 406.5 %copy-start.1 = (f32[448,256]{1,0:T(8,128)S(1)}, f32[448,256]{1,0:T(8,128)}, u32[]{:S(2)}) copy-start(f32[448,256]{1,0:T(8,128)} %all-reduce.33.cloned.1.call-done) | copy-start | bytes 1376260
Sparse Core Ops, SparseCore 0:
  28.8 35.7 all-reduce.32
  68.5 71.0 all-reduce.34
where the time goes:
time: 921 us; the launch traced here: 916 us
  local copies, waits for them, and re-layouts  312 us (34%)
  matrix products  221 us (24%)
  loops' own time  184 us (20%)
  waiting for transfers between devices  108 us (12%)
  other arithmetic  75.4 us (8%)
  between operations  14.7 us (2%)
    dot_general x317, matrix products, high_dot(): jnp.dot(left, right, precision=lax.Precision.HIGHEST, preferred_element_t...  216 us
    another operation x16, loops' own time, cholesky_small(): lax.fori_loop(0, order, column_step, (matrix, jnp.zeros_like(matrix)))[1]  184 us
    dynamic_slice x256, local copies, waits for them, and re-layouts, row_step(): pivot = lax.dynamic_slice_in_dim(row_lower, index, 1, 0)[0]  151 us
    dynamic_slice x256, local copies, waits for them, and re-layouts, column_step(): pivot = jnp.sqrt(lax.dynamic_slice_in_dim(column, index, 1, 0)[0])  150 us
    psum x1, waiting for transfers between devices, body(): lower, inverse = cholesky_pair(lax.psum(gram, 'dom'))  71.8 us
    psum x1, waiting for transfers between devices, body(): coeffs = lax.psum(project(weighted, pose_bin, panels), 'rows')  35.7 us
    add x256, other arithmetic, row_step(): return inverse + unit[:, None] * solved[None, :]  19.7 us
    add x256, other arithmetic, column_step(): lower + filled[:, None] * (places == index).astype(matrix.dtype)[None, :]  19.3 us
  transfers between devices with their start and end apart: 2, of which 2 were waited for; matrix products, arithmetic and copies ran while one was open for 0% of the time, Pallas kernels for 0%

commit v1 on v0

v1 whole, which is shorter than its diff:
```python
import functools

import jax
import jax.numpy as jnp
from jax import lax
from jax.experimental import pallas as pl
from jax.experimental.pallas import tpu as pltpu
from jax.sharding import PartitionSpec as P

F32 = jnp.float32
BF16 = jnp.bfloat16


def dot_f32(left, right, dims):
    return lax.dot_general(
        left, right, (dims, ((), ())), precision=lax.Precision.HIGHEST, preferred_element_type=F32
    )


def widen(column, lanes):
    return jnp.concatenate([column] * (lanes // 128), axis=1)


def project_kernel(groups, steps, images, panels, means, table, pose, group, out, pick, mask, acc):
    step = pl.program_id(0)
    rows, chunk = images.shape

    @pl.when(step == 0)
    def _():
        place = lax.broadcasted_iota(jnp.int32, (128, rows), 0)
        hot = (place % groups == group[...]) & (place < 3 * groups)
        pick[...] = jnp.transpose(hot.astype(F32)).astype(BF16)
        mask[...] = jnp.transpose(jnp.broadcast_to(pose[...].astype(F32), (128, rows)))
        acc[...] = jnp.zeros_like(acc)

    exact = table[...]
    high = exact.astype(BF16)
    left = exact - high.astype(F32)
    mid = left.astype(BF16)
    low = (left - mid.astype(F32)).astype(BF16)
    fill = jnp.zeros((128 - 3 * groups, chunk), BF16)
    parts = jnp.concatenate([high, mid, low, fill], axis=0)
    ctf = jnp.dot(pick[...], parts, preferred_element_type=F32)
    second = widen(mask[...], chunk) > 0.5
    mean = jnp.where(second, means[1:2, :], means[0:1, :])
    weighted = (ctf * (images[...].astype(F32) - ctf * mean)).astype(BF16)
    for which in range(2):
        acc[which] += jnp.dot(weighted, panels[which], preferred_element_type=F32)

    @pl.when(step == steps - 1)
    def _():
        out[...] = jnp.where(widen(mask[...], out.shape[1]) > 0.5, acc[1], acc[0])


def project(images, panels, means, table, pose, group):
    rows, pixels = images.shape
    bins, _, probes = panels.shape
    groups = table.shape[0]
    chunk = 1280 if pixels % 1280 == 0 else 128
    steps = pixels // chunk
    return pl.pallas_call(
        functools.partial(project_kernel, groups, steps),
        grid=(steps,),
        in_specs=[
            pl.BlockSpec((rows, chunk), lambda i: (0, i)),
            pl.BlockSpec((bins, chunk, probes), lambda i: (0, i, 0)),
            pl.BlockSpec((bins, chunk), lambda i: (0, i)),
            pl.BlockSpec((groups, chunk), lambda i: (0, i)),
            pl.BlockSpec((1, rows), lambda i: (0, 0)),
            pl.BlockSpec((1, rows), lambda i: (0, 0)),
        ],
        out_specs=pl.BlockSpec((rows, probes), lambda i: (0, 0)),
        out_shape=jax.ShapeDtypeStruct((rows, probes), F32),
        scratch_shapes=[
            pltpu.VMEM((rows, 128), BF16),
            pltpu.VMEM((rows, 128), F32),
            pltpu.VMEM((bins, rows, probes), F32),
        ],
        compiler_params=pltpu.CompilerParams(vmem_limit_bytes=60 * 2**20),
        name="project",
    )(images, panels, means, table, pose.reshape(1, rows), group.reshape(1, rows))


SIZE = 64
PANEL = 4


def factor_block(block):
    lane = lax.broadcasted_iota(jnp.int32, (8, 2 * SIZE), 1)
    sub = lax.broadcasted_iota(jnp.int32, (8, 2 * SIZE), 0)
    tiles = []
    for t in range(SIZE // 8):
        unit = (lane == sub + (8 * t + SIZE)).astype(F32)
        part = jnp.concatenate([block[8 * t : 8 * t + 8], jnp.zeros((8, SIZE), F32)], axis=1)
        tiles.append(part + unit)
    count = len(tiles)
    pivots = [jnp.ones((8, 2 * SIZE), F32) for _ in range(count)]
    for base in range(0, SIZE, PANEL):
        first = base // 8
        cols = [
            [None] * first
            + [jnp.broadcast_to(tiles[t][:, base + j : base + j + 1], (8, 2 * SIZE)) for t in range(first, count)]
            for j in range(PANEL)
        ]
        for j in range(PANEL):
            k = base + j
            row = k % 8
            pivot = cols[j][first][row : row + 1]
            inverse = 1.0 / pivot
            pivots[first] = jnp.where(sub == row, pivot, pivots[first])
            scale = [None] * count
            for t in range(first, count):
                scale[t] = cols[j][t] * inverse
            scale[first] = jnp.where(sub > row, scale[first], 0.0)
            for later in range(j + 1, PANEL):
                value = cols[later][first][row : row + 1]
                for t in range(first, count):
                    cols[later][t] = cols[later][t] - scale[t] * value
            line = tiles[first][row : row + 1]
            for t in range(first, count):
                tiles[t] = tiles[t] - scale[t] * line
    done = []
    for t in range(count):
        keep = (lane >= SIZE) | (lane >= sub + 8 * t)
        done.append(jnp.where(keep, tiles[t] * lax.rsqrt(pivots[t]), 0.0))
    return jnp.concatenate(done, axis=0)


def finish_kernel(particles, gram, coeffs, scores, factor, work, side):
    order = gram.shape[0]
    work[...] = gram[...] * (1.0 / particles)
    spot = lax.broadcasted_iota(jnp.int32, (order, order), 0)
    side[...] = (spot == lax.broadcasted_iota(jnp.int32, (order, order), 1)).astype(F32)
    for start in range(0, order, SIZE):
        stop = start + SIZE
        both = factor_block(work[start:stop, start:stop])
        upper, lower = both[:, :SIZE], both[:, SIZE:]
        if start:
            factor[start:stop, :start] = jnp.zeros((SIZE, start), F32)
        factor[start:stop, start:stop] = upper
        reach = -(-stop // 128) * 128
        row_side = dot_f32(lower, side[start:stop, :reach], ((1,), (0,)))
        side[start:stop, :reach] = row_side
        if stop < order:
            from_col = stop // 128 * 128
            row_work = dot_f32(lower, work[start:stop, from_col:], ((1,), (0,)))
            right = row_work[:, stop - from_col :]
            factor[start:stop, stop:] = right
            work[stop:, from_col:] = work[stop:, from_col:] - dot_f32(right, row_work, ((0,), (0,)))
            side[stop:, :reach] = side[stop:, :reach] - dot_f32(right, row_side, ((0,), (0,)))
    scores[...] = dot_f32(coeffs[...], side[...], ((1,), (1,)))


def finish(gram, coeffs, particles):
    order = gram.shape[0]
    return pl.pallas_call(
        functools.partial(finish_kernel, particles),
        in_specs=[pl.BlockSpec(memory_space=pltpu.VMEM)] * 2,
        out_specs=[pl.BlockSpec(memory_space=pltpu.VMEM)] * 2,
        out_shape=[jax.ShapeDtypeStruct(coeffs.shape, F32), jax.ShapeDtypeStruct((order, order), F32)],
        scratch_shapes=[pltpu.VMEM((order, order), F32)] * 2,
        name="finish",
    )(gram, coeffs)


MESH = pl.DeviceIdType.MESH
CHUNKS = 4


def combine_kernel(n_rows, n_dom, part, coeffs, gram, near, far, held, wide, give, take, *sems):
    pair_send, pair_recv, far_send, far_recv, back_send, back_recv = sems[:6]
    dom_send, dom_recv, all_send, all_recv, row_send, row_recv = sems[6:]
    row, dom = lax.axis_index("rows"), lax.axis_index("dom")
    side, pair = row % 2, row // 2
    other = 1 - side
    partner = pair * 2 + other
    across = (1 - pair) * 2 + side
    half = part.shape[0] // 2
    size = half // CHUNKS
    order = part.shape[1]
    slab = order // n_rows
    piece = slab // n_dom

    def to(source, target, send, recv, place):
        return pltpu.make_async_remote_copy(
            src_ref=source, dst_ref=target, send_sem=send, recv_sem=recv, device_id=place, device_id_type=MESH
        )

    barrier = pltpu.get_barrier_semaphore()
    for step in range(1, n_rows):
        pl.semaphore_signal(barrier, inc=1, device_id=(dom, (row + step) % n_rows), device_id_type=MESH)
    for step in range(1, n_dom):
        pl.semaphore_signal(barrier, inc=1, device_id=((dom + step) % n_dom, row), device_id_type=MESH)
    pl.semaphore_wait(barrier, n_rows + n_dom - 2)

    def mine(start, chunk):
        return pl.ds(pl.multiple_of(start * half + chunk * size, 8), size)

    first = []
    for c in range(CHUNKS):
        first.append(
            to(part.at[mine(other, c)], near.at[c], pair_send.at[c], pair_recv.at[c], (dom, partner))
        )
        first[c].start()
    second = []
    for c in range(CHUNKS):
        first[c].wait_recv()
        held[c] = part[mine(side, c), :] + near[c]
        second.append(to(held.at[c], far.at[c], far_send.at[c], far_recv.at[c], (dom, across)))
        second[c].start()
    third = []
    for c in range(CHUNKS):
        second[c].wait_recv()
        coeffs[mine(side, c), :] = held[c] + far[c]
        ours = coeffs.at[mine(side, c)]
        third.append(to(ours, ours, back_send.at[c], back_recv.at[c], (dom, partner)))
        third[c].start()

    span = max(slab, 128)
    columns = pl.ds(pl.multiple_of(row * slab // span * span, 128), span)

    def square(start):
        rows = pl.ds(pl.multiple_of(start * half, 8), half)
        return dot_f32(coeffs[rows, columns], coeffs[rows, :], ((0,), (0,)))

    wide[...] = square(side)
    for c in range(CHUNKS):
        third[c].wait_recv()
    wide[...] = wide[...] + square(other)
    ours = wide[pl.ds(pl.multiple_of(row * slab % span, 8), slab), :]
    for d in range(n_dom):
        give[d] = ours[d * piece : (d + 1) * piece, :]

    out = []
    for step in range(1, n_dom):
        there = (dom + step) % n_dom
        out.append(
            to(give.at[there], take.at[dom], dom_send.at[step - 1], dom_recv.at[step - 1], (there, row))
        )
        out[-1].start()
    take[dom] = give[dom]
    for copy in out:
        copy.wait_recv()
    total = take[0]
    for d in range(1, n_dom):
        total = total + take[d]
    gram[row, dom] = total

    spread = []
    for step in range(1, n_dom):
        there = (dom + step) % n_dom
        block = gram.at[row, dom]
        spread.append(to(block, block, all_send.at[step - 1], all_recv.at[step - 1], (there, row)))
        spread[-1].start()
    for copy in spread:
        copy.wait_recv()
    last = []
    for step in range(1, n_rows):
        there = (row + step) % n_rows
        block = gram.at[row]
        last.append(to(block, block, row_send.at[step - 1], row_recv.at[step - 1], (dom, there)))
        last[-1].start()
    for copy in last:
        copy.wait_recv()
    for copy in first + second + third + out + spread + last:
        copy.wait_send()


def combine(part):
    n_rows, n_dom = lax.axis_size("rows"), lax.axis_size("dom")
    count, order = part.shape
    slab = order // n_rows
    piece = slab // n_dom
    size = count // 2 // CHUNKS
    dma = pltpu.SemaphoreType.DMA
    coeffs, gram = pl.pallas_call(
        functools.partial(combine_kernel, n_rows, n_dom),
        in_specs=[pl.BlockSpec(memory_space=pltpu.VMEM)],
        out_specs=[pl.BlockSpec(memory_space=pltpu.VMEM)] * 2,
        out_shape=[
            jax.ShapeDtypeStruct((count, order), F32),
            jax.ShapeDtypeStruct((n_rows, n_dom, piece, order), F32),
        ],
        scratch_shapes=[
            pltpu.VMEM((CHUNKS, size, order), F32),
            pltpu.VMEM((CHUNKS, size, order), F32),
            pltpu.VMEM((CHUNKS, size, order), F32),
            pltpu.VMEM((max(slab, 128), order), F32),
            pltpu.VMEM((n_dom, piece, order), F32),
            pltpu.VMEM((n_dom, piece, order), F32),
        ]
        + [dma((CHUNKS,))] * 6
        + [dma((n_dom - 1,))] * 4
        + [dma((n_rows - 1,))] * 2,
        compiler_params=pltpu.CompilerParams(collective_id=0, has_side_effects=True),
        name="combine",
    )(part)
    return coeffs, gram.reshape(order, order)


def body(images, panels, mean_panels, ctf_table, pose_bin, ctf_group):
    particles = images.shape[0] * lax.axis_size("dom")
    coeffs, gram = combine(project(images, panels, mean_panels, ctf_table, pose_bin, ctf_group))
    return tuple(finish(gram, coeffs, particles))


def solution(mesh):
    placed = (
        P("dom", "rows"),
        P("dom", "rows", None),
        P("dom", "rows"),
        P(None, "rows"),
        P("dom"),
        P("dom"),
    )
    return jax.shard_map(
        body, mesh=mesh, in_specs=placed, out_specs=(P("dom", None), P()), check_vma=False
    )
```

time: 921 us -> 55.1 us (0.06)
  local copies, waits for them, and re-layouts: 312 us -> 0 us
  matrix products: 221 us -> 0 us
  loops' own time: 184 us -> 0 us
  waiting for transfers between devices: 108 us -> 0 us
  other arithmetic: 75.4 us -> 0 us
  Pallas kernels: 0 us -> 54.2 us
  between operations: 14.7 us -> 0.64 us
    dynamic_slice x512 -> x0, local copies, waits for them, and re-layouts: 301 us -> none  [the longest x256 151 us: row_step(): pivot = lax.dynamic_slice_in_dim(row_lower, index, 1, 0)[0]]
    dot_general x320 -> x0, matrix products: 221 us -> none  [the longest x317 216 us: high_dot(): jnp.dot(left, right, precision=lax.Precision.HIGHEST, preferred_element_t...]
    another operation x32 -> x0, loops' own time: 184 us -> none  [the longest x16 184 us: cholesky_small(): lax.fori_loop(0, order, column_step, (matrix, jnp.zeros_like(matrix)))[1]]
    psum x2 -> x0, waiting for transfers between devices: 107 us -> none  [the longest x1 71.8 us: body(): lower, inverse = cholesky_pair(lax.psum(gram, 'dom'))]
    pallas_call x0 -> x3, Pallas kernels: none -> 54.2 us  [the longest x1 29.1 us: combine(): pl.pallas_call(functools.partial(combine_kernel, n_rows, n_dom), in_specs...]
    add x512 -> x0, other arithmetic: 39 us -> none  [the longest x256 19.7 us: row_step(): return inverse + unit[:, None] * solved[None, :]]
    sub x256 -> x0, other arithmetic: 18.9 us -> none  [column_step(): work = work - below[:, None] * below[None, :]]
    convert_element_type x513 -> x0, other arithmetic: 9.5 us -> none  [the longest x1 7.75 us: weighted_rows(): (ctf_rows * (images.astype(jnp.float32) - ctf_rows * mean_rows)).astype(j...]
  transfers between devices with their start and end apart: 2 -> 0, of which waited for: 2 -> 0; matrix products, arithmetic and copies ran while one was open for 0% -> 0% of each run, Pallas kernels for 0% -> 0%
where the time goes in v1:
time: 55.1 us; the launch traced here: 54.8 us
  Pallas kernels  54.2 us (98%)
  between operations  0.64 us (1%)
    pallas_call x1, Pallas kernels, combine(): pl.pallas_call(functools.partial(combine_kernel, n_rows, n_dom), in_specs...  29.1 us
    pallas_call x1, Pallas kernels, finish(): pl.pallas_call(functools.partial(finish_kernel, particles), in_specs=[pl....  15.6 us
    pallas_call x1, Pallas kernels, project(): pl.pallas_call(functools.partial(project_kernel, groups, steps), grid=(st...  9.48 us

profile of v1, /device:TPU:0, one launch (start us, length us, event | category | flops | bytes accessed | tf_op | source)
XLA Modules:
  0.0 54.8 jit_solution(9845521828552830153)
XLA Ops:
  0.6 9.5 %project.1.part = f32[448,256]{1,0:T(8,128)} custom-call(bf16[448,6400]{1,0:T(8,128)(2,1)} %images.1, bf16[2,6400,256]{2,1,0:T(8,128)(2,1)} %panels.1, f32[2,6400]{1,0:T(2,128)} %means.1, f32[16,6400]{1,0:T(8,128)} %table.1, s32[1,448]{1,0:T(1,128)} %bitcast.4, s32[1,448]{1,0:T(1,128)} %bitcast.5), custom_call_target="tpu_custom_call" | custom-call | tf_op jit(solution)/shard_map/project/pallas_call | solution.py:61
  10.1 29.1 %combine.1 = (f32[448,256]{1,0:T(8,128)}, f32[4,8,8,256]{3,2,1,0:T(8,128)}) custom-call(f32[448,256]{1,0:T(8,128)} %project.1.part), custom_call_target="tpu_custom_call" | custom-call | tf_op jit(solution)/shard_map/combine/pallas_call | solution.py:276
  39.3 15.6 %finish.1 = (f32[448,256]{1,0:T(8,128)}, f32[256,256]{1,0:T(8,128)}) custom-call(f32[256,256]{1,0:T(8,128)} %bitcast.3, f32[448,256]{1,0:T(8,128)} %get-tuple-element.5.coeffs), custom_call_target="tpu_custom_call" | custom-call | tf_op jit(solution)/shard_map/finish/pallas_call | solution.py:156

commit v2 on v1

--- a/solution.py
+++ b/solution.py
@@ -82,7 +82,7 @@
 
 
 SIZE = 64
-PANEL = 4
+PANEL = 16
 
 
 def factor_block(block):
@@ -104,20 +104,20 @@
         ]
         for j in range(PANEL):
             k = base + j
-            row = k % 8
-            pivot = cols[j][first][row : row + 1]
+            row, here = k % 8, k // 8
+            pivot = cols[j][here][row : row + 1]
             inverse = 1.0 / pivot
-            pivots[first] = jnp.where(sub == row, pivot, pivots[first])
+            pivots[here] = jnp.where(sub == row, pivot, pivots[here])
             scale = [None] * count
-            for t in range(first, count):
+            for t in range(here, count):
                 scale[t] = cols[j][t] * inverse
-            scale[first] = jnp.where(sub > row, scale[first], 0.0)
+            scale[here] = jnp.where(sub > row, scale[here], 0.0)
             for later in range(j + 1, PANEL):
-                value = cols[later][first][row : row + 1]
-                for t in range(first, count):
+                value = cols[later][here][row : row + 1]
+                for t in range(here, count):
                     cols[later][t] = cols[later][t] - scale[t] * value
-            line = tiles[first][row : row + 1]
-            for t in range(first, count):
+            line = tiles[here][row : row + 1]
+            for t in range(here, count):
                 tiles[t] = tiles[t] - scale[t] * line
     done = []
     for t in range(count):
@@ -246,20 +246,24 @@
         total = total + take[d]
     gram[row, dom] = total
 
-    spread = []
+    def relay(owner, slot):
+        block = gram.at[row, owner]
+        for step in range(1, n_rows):
+            there = (row + step) % n_rows
+            place = (step - 1, slot)
+            last.append(to(block, block, row_send.at[place], row_recv.at[place], (dom, there)))
+            last[-1].start()
+
+    spread, last = [], []
     for step in range(1, n_dom):
         there = (dom + step) % n_dom
         block = gram.at[row, dom]
         spread.append(to(block, block, all_send.at[step - 1], all_recv.at[step - 1], (there, row)))
         spread[-1].start()
-    for copy in spread:
-        copy.wait_recv()
-    last = []
-    for step in range(1, n_rows):
-        there = (row + step) % n_rows
-        block = gram.at[row]
-        last.append(to(block, block, row_send.at[step - 1], row_recv.at[step - 1], (dom, there)))
-        last[-1].start()
+    relay(dom, 0)
+    for step in range(1, n_dom):
+        spread[step - 1].wait_recv()
+        relay((dom - step + n_dom) % n_dom, step)
     for copy in last:
         copy.wait_recv()
     for copy in first + second + third + out + spread + last:
@@ -291,7 +295,7 @@
         ]
         + [dma((CHUNKS,))] * 6
         + [dma((n_dom - 1,))] * 4
-        + [dma((n_rows - 1,))] * 2,
+        + [dma((n_rows - 1, n_dom))] * 2,
         compiler_params=pltpu.CompilerParams(collective_id=0, has_side_effects=True),
         name="combine",
     )(part)

time: 55.1 us -> 50.9 us (0.924)
  Pallas kernels: 54.2 us -> 50 us
    pallas_call x1, Pallas kernels: 15.6 us -> 10.6 us  [finish(): pl.pallas_call(functools.partial(finish_kernel, particles), in_specs=[pl....]
    pallas_call x1, Pallas kernels: 29.1 us -> 30 us  [combine(): pl.pallas_call(functools.partial(combine_kernel, n_rows, n_dom), in_specs...]
where the time goes in v2:
time: 50.9 us; the launch traced here: 50.7 us
  Pallas kernels  50 us (98%)
  between operations  0.64 us (1%)
    pallas_call x1, Pallas kernels, combine(): pl.pallas_call(functools.partial(combine_kernel, n_rows, n_dom), in_specs...  30 us
    pallas_call x1, Pallas kernels, finish(): pl.pallas_call(functools.partial(finish_kernel, particles), in_specs=[pl....  10.6 us
    pallas_call x1, Pallas kernels, project(): pl.pallas_call(functools.partial(project_kernel, groups, steps), grid=(st...  9.48 us

profile of v2, /device:TPU:0, one launch (start us, length us, event | category | flops | bytes accessed | tf_op | source)
XLA Modules:
  0.0 50.7 jit_solution(9019672419575026994)
XLA Ops:
  0.6 9.5 %project.1.part = f32[448,256]{1,0:T(8,128)} custom-call(bf16[448,6400]{1,0:T(8,128)(2,1)} %images.1, bf16[2,6400,256]{2,1,0:T(8,128)(2,1)} %panels.1, f32[2,6400]{1,0:T(2,128)} %means.1, f32[16,6400]{1,0:T(8,128)} %table.1, s32[1,448]{1,0:T(1,128)} %bitcast.4, s32[1,448]{1,0:T(1,128)} %bitcast.5), custom_call_target="tpu_custom_call" | custom-call | tf_op jit(solution)/shard_map/project/pallas_call | solution.py:61
  10.1 30.0 %combine.1 = (f32[448,256]{1,0:T(8,128)}, f32[4,8,8,256]{3,2,1,0:T(8,128)}) custom-call(f32[448,256]{1,0:T(8,128)} %project.1.part), custom_call_target="tpu_custom_call" | custom-call | tf_op jit(solution)/shard_map/combine/pallas_call | solution.py:280
  40.1 10.6 %finish.1 = (f32[448,256]{1,0:T(8,128)}, f32[256,256]{1,0:T(8,128)}) custom-call(f32[256,256]{1,0:T(8,128)} %bitcast.3, f32[448,256]{1,0:T(8,128)} %get-tuple-element.5.coeffs), custom_call_target="tpu_custom_call" | custom-call | tf_op jit(solution)/shard_map/finish/pallas_call | solution.py:156
